TPU v7x, 256 devices: a whole 4x4x8 slice. The times are simulated.
256 devices in a mesh: gx: 32 (over z, x), gy: 8 (over y, core).
Axes of the slice: x: 4, y: 4, z: 8, core: 2. Of those that a mesh axis runs over, the one named last changes fastest.
Arguments:
- right_side: float32 [8192, 512], P(('gx', 'gy')), may hold values from -6 to 6
- diagonal: float32 [8192, 512], P(('gx', 'gy')), may hold values from 0.5 to 2
- features: float32 [8192, 64, 512], P(('gx', 'gy')), may hold values from -0.078125 to 0.078125
- neighbours: int32 [8192, 27], P(('gx', 'gy')), may hold values from -1 to 8191, as said below
- vertex_features: float32 [64, 262144], P(None, ('gx', 'gy')), may hold values from -0.75 to 0.75
- vertex_bricks: int32 [262144], P(('gx', 'gy')), may hold values from 0 to 8191, as said below
Outputs:
- solution_field: float32 [8192, 512], P(('gx', 'gy'))
- residual: float32 [8192, 512], P(('gx', 'gy'))
- vertex_values: float32 [262144], P(('gx', 'gy'))
Inputs may be any that keep to these rules, and one draw needn't show every extreme that they name: `neighbours`: bricks sit at distinct integer brick coordinates; slot k of a row names the brick at the offset (k // 9 - 1, k // 3 % 3 - 1, k % 3 - 1) from its own, or -1 where no brick is there, so slot 13 names the brick itself and the relation is symmetric. Every brick whose coordinates differ from a brick's by at most two in each direction is held by a device whose gx and gy indices each differ from that brick's holder's by at most one. `vertex_bricks`: vertex n names a brick of its own gx slab: a brick from (n // 8192) * 256 to (n // 8192) * 256 + 255.
All inputs are finite; a program needn't handle non-finite values.
Results may differ from a plain program's by a relative error of at most 0.0002.
Values sent between devices are 32-bit elements; how exact they have to be, the bound alone decides.
No kernel may reach another device: no remote copies, remote signals or barrier semaphores. Data moves between devices by JAX's collectives and lax.ppermute only.
A program may use at most 64 MiB of HBM per device.

v0:
```python
import jax
import jax.numpy as jnp
from jax import lax
from jax.sharding import PartitionSpec as P

ITERS = 3


def with_halo(cells, sides, width):
    for axis, dim in sides:
        count = lax.axis_size(axis)
        ends = count - 1
        head = lax.slice_in_dim(cells, 0, width, axis=dim)
        tail = lax.slice_in_dim(cells, cells.shape[dim] - width, cells.shape[dim], axis=dim)
        cells = jnp.concatenate(
            [
                lax.ppermute(tail, axis, [(i, (i + 1) % count) for i in range(ends)]),
                cells,
                lax.ppermute(head, axis, [((i + 1) % count, i) for i in range(ends)]),
            ],
            axis=dim,
        )
    return cells


def coefficient(features, field):
    return jnp.einsum("bfv,bv->bf", features, field, precision=lax.Precision.HIGHEST)


def squares(values):
    return lax.psum(jnp.sum(values * values), ("gx", "gy"))


def per_device(right_side, diagonal, features, neighbours, vertex_features, vertex_bricks):
    nrows = features.shape[0]
    width = features.shape[1]
    across = lax.axis_size("gy")
    row_index = lax.axis_index("gx")
    col_index = lax.axis_index("gy")
    targets = jnp.arange(9 * nrows, dtype=jnp.int32)
    valid = neighbours >= 0
    safe_ids = jnp.where(valid, neighbours, 0)
    owner = safe_ids // nrows
    offset_x = owner // across - row_index + 1
    offset_y = owner % across - col_index + 1
    inside = valid & (offset_x >= 0) & (offset_x < 3) & (offset_y >= 0) & (offset_y < 3)
    position, inside = ((offset_x * 3 + offset_y) * nrows + safe_ids % nrows, inside)
    hits = (position[:, :, None] == targets[None, None, :]) & inside[:, :, None]
    counts = jnp.sum(hits.astype(jnp.float32), axis=1)

    def first_halo(values):
        cycle = with_halo(values.reshape(1, 1, nrows, width), (("gx", 0), ("gy", 1)), 1)
        return cycle.reshape(9 * nrows, width)

    def first_sum(values):
        return jnp.dot(counts, first_halo(values), precision=lax.Precision.HIGHEST)

    solution_field = jnp.zeros_like(right_side)
    residual = right_side
    direction = right_side
    norm_now = squares(residual)
    for step in range(ITERS):
        second_cycle = with_halo(
            first_sum(coefficient(features, direction)).reshape(1, 1, nrows, width),
            (("gx", 0), ("gy", 1)),
            1,
        )
        second = jnp.dot(
            counts, second_cycle.reshape(9 * nrows, width), precision=lax.Precision.HIGHEST
        )
        image = diagonal * direction + jnp.einsum(
            "bfv,bf->bv", features, second, precision=lax.Precision.HIGHEST
        )
        alpha = norm_now / lax.psum(jnp.sum(direction * image), ("gx", "gy"))
        solution_field = solution_field + alpha * direction
        residual = residual - alpha * image
        norm_next = squares(residual)
        direction = residual + norm_next / norm_now * direction
        norm_now = norm_next
    surface = first_sum(coefficient(features, solution_field))
    slab_rows = lax.all_gather(surface, "gy", axis=0, tiled=True)
    local_ids = vertex_bricks - row_index * across * nrows
    picked = jnp.take(slab_rows, local_ids, axis=0)
    vertex_values = jnp.sum(vertex_features * picked.T, axis=0)
    return (solution_field, residual, vertex_values)


def solution(mesh):
    placed = (
        P(("gx", "gy"), None),
        P(("gx", "gy"), None),
        P(("gx", "gy"), None, None),
        P(("gx", "gy"), None),
        P(None, ("gx", "gy")),
        P(("gx", "gy")),
    )
    return jax.shard_map(
        per_device,
        mesh=mesh,
        in_specs=placed,
        out_specs=(P(("gx", "gy"), None), P(("gx", "gy"), None), P(("gx", "gy"))),
        check_vma=False,
    )
```

profile of v0, /device:TPU:129, one launch (start us, length us, event | category | flops | bytes accessed | tf_op | source)
XLA Modules:
  0.0 560.7 jit_solution(662496368784365687)
XLA Ops:
  0.7 5.8 %fusion.8 = f32[32,1,64]{2,1,0:T(1,128)S(1)} fusion(f32[32,64,512]{2,1,0:T(8,128)} %param.8, f32[32,512,1]{1,0,2:T(8,128)} %bitcast.92), kind=kOutput, calls=%fused_computation.25 | convolution fusion | flops 12582912 | bytes 4268032 | tf_op jit(solution)/shard_map/bfv,bv->bf/dot_general | solution.py:27
  12.7 5.6 collective-permute-done
  18.2 4.0 collective-permute-start.3
  32.1 4.4 collective-permute-done.4
  38.6 5.2 collective-permute-start.6
  45.2 4.3 fusion.25
  50.2 74.5 %all-reduce = (f32[]{:T(128)}, f32[]{:T(128)}) all-reduce(f32[]{:T(128)} %get-tuple-element.4, f32[]{:T(128)} %get-tuple-element.3), channel_id=1, replica_groups=mesh['gx'=32,'gy'=8] {'gx','gy'}, use_global_device_ids=true, to_apply=%region_1.2 | all-reduce | flops 2 | bytes 16 | tf_op jit(solution)/shard_map/psum | solution.py:31
  126.7 73.5 %psum.44 = f32[]{:T(128)} all-reduce(f32[]{:T(128)} %get-tuple-element.9), channel_id=1, replica_groups=mesh['gx'=32,'gy'=8] {'gx','gy'}, use_global_device_ids=true, to_apply=%region_6.7 | all-reduce | flops 1 | bytes 8 | tf_op jit(solution)/shard_map/psum | solution.py:31
  201.5 5.4 fusion.6
  212.7 5.9 %collective-permute-done.8 = f32[1,1,32,64]{3,2,1,0:T(8,128)S(1)} collective-permute-done((f32[1,1,32,64]{3,2,1,0:T(8,128)S(1)}, f32[1,1,32,64]{3,2,1,0:T(8,128)S(1)}, u32[]{:S(2)}, u32[]{:S(2)}) %collective-permute-start.8) | collective-permute-done | bytes 8224 | tf_op jit(solution)/shard_map/ppermute | solution.py:17
  218.6 4.0 collective-permute-start.11
  231.3 4.4 collective-permute-done.12
  238.9 4.3 collective-permute-start.14
  247.1 73.2 %psum.45 = f32[]{:T(128)} all-reduce(f32[]{:T(128)} %multiply_reduce_fusion.2), channel_id=1, replica_groups=mesh['gx'=32,'gy'=8] {'gx','gy'}, use_global_device_ids=true, to_apply=%region_8.9 | all-reduce | flops 1 | bytes 8 | tf_op jit(solution)/shard_map/psum | solution.py:74
  322.3 73.3 %psum.46 = f32[]{:T(128)} all-reduce(f32[]{:T(128)} %get-tuple-element.7), channel_id=1, replica_groups=mesh['gx'=32,'gy'=8] {'gx','gy'}, use_global_device_ids=true, to_apply=%region_10.11 | all-reduce | flops 1 | bytes 8 | tf_op jit(solution)/shard_map/psum | solution.py:31
  397.0 5.4 fusion.4
  402.4 4.2 collective-permute-start.17
  408.6 5.9 %collective-permute-done.16 = f32[1,1,32,64]{3,2,1,0:T(8,128)S(1)} collective-permute-done((f32[1,1,32,64]{3,2,1,0:T(8,128)S(1)}, f32[1,1,32,64]{3,2,1,0:T(8,128)S(1)}, u32[]{:S(2)}, u32[]{:S(2)}) %collective-permute-start.16) | collective-permute-done | bytes 8224 | tf_op jit(solution)/shard_map/ppermute | solution.py:17
  427.1 4.4 collective-permute-done.20
  434.8 4.1 collective-permute-start.22
  443.0 73.2 %psum.47 = f32[]{:T(128)} all-reduce(f32[]{:T(128)} %multiply_reduce_fusion), channel_id=1, replica_groups=mesh['gx'=32,'gy'=8] {'gx','gy'}, use_global_device_ids=true, to_apply=%region_12.13 | all-reduce | flops 1 | bytes 8 | tf_op jit(solution)/shard_map/psum | solution.py:74
  518.2 5.3 fusion.2
  529.2 5.8 %collective-permute-done.24 = f32[1,1,32,64]{3,2,1,0:T(8,128)S(1)} collective-permute-done((f32[1,1,32,64]{3,2,1,0:T(8,128)S(1)}, f32[1,1,32,64]{3,2,1,0:T(8,128)S(1)}, u32[]{:S(2)}, u32[]{:S(2)}) %collective-permute-start.24) | collective-permute-done | bytes 8224 | tf_op jit(solution)/shard_map/ppermute | solution.py:17
  543.8 13.1 %all_gather.3 = f32[256,64]{1,0:T(8,128)S(1)} all-gather(f32[32,64]{1,0:T(8,128)S(1)} %fusion.30), channel_id=1, replica_groups=mesh['gx'=32,'gy'=8] {'gy'}, dimensions={0}, use_global_device_ids=true | all-gather | bytes 73728 | tf_op jit(solution)/shard_map/all_gather | solution.py:81
  (100 shorter events, 83.5 us)
Async XLA Ops:
  6.5 6.2 %collective-permute-start.1 = (f32[1,1,32,64]{3,2,1,0:T(8,128)S(1)}, f32[1,1,32,64]{3,2,1,0:T(8,128)S(1)}, u32[]{:S(2)}, u32[]{:S(2)}) collective-permute-start(f32[1,1,32,64]{3,2,1,0:T(8,128)S(1)} %bitcast.101), channel_id=1, source_target_pairs={{8,0},{16,8},{24,16},{32,24},{40,32},{48,40},{56,48},{64,56},{72,6... | collective-permute-start | bytes 24584 | tf_op jit(solution)/shard_map/ppermute | solution.py:19
  10.4 7.8 %collective-permute-start = (f32[1,1,32,64]{3,2,1,0:T(8,128)S(1)}, f32[1,1,32,64]{3,2,1,0:T(8,128)S(1)}, u32[]{:S(2)}, u32[]{:S(2)}) collective-permute-start(f32[1,1,32,64]{3,2,1,0:T(8,128)S(1)} %bitcast.102), channel_id=1, source_target_pairs={{0,8},{8,16},{16,24},{24,32},{32,40},{40,48},{48,56},{56,64},{64,7... | collective-permute-start | bytes 24584 | tf_op jit(solution)/shard_map/ppermute | solution.py:17
  18.2 7.4 %collective-permute-start.3 = (f32[3,1,32,64]{3,2,1,0:T(8,128)S(1)}, f32[3,1,32,64]{3,2,1,0:T(8,128)S(1)}, u32[]{:S(2)}, u32[]{:S(2)}) collective-permute-start(f32[3,1,32,64]{3,2,1,0:T(8,128)S(1)} %pad_maximum_fusion.7), channel_id=1, source_target_pairs={{1,0},{2,1},{3,2},{4,3},{5,4},{6,5},{7,6},{9,8},{10,9},{11,10},{12... | collective-permute-start | bytes 73736 | tf_op jit(solution)/shard_map/ppermute | solution.py:19
  26.8 5.3 collective-permute-start.5
  28.7 7.8 %collective-permute-start.4 = (f32[1,1,32,64]{3,2,1,0:T(8,128)S(1)}, f32[1,1,32,64]{3,2,1,0:T(8,128)S(1)}, u32[]{:S(2)}, u32[]{:S(2)}) collective-permute-start(f32[1,1,32,64]{3,2,1,0:T(8,128)S(1)} %convolution_bitcast_fusion.2), channel_id=1, source_target_pairs={{0,8},{8,16},{16,24},{24,32},{32,40},{40,48},{48,56},{56,64},{64,7... | collective-permute-start | bytes 24584 | tf_op jit(solution)/shard_map/ppermute | solution.py:17
  36.5 7.3 %collective-permute-start.7 = (f32[3,1,32,64]{3,2,1,0:T(8,128)S(1)}, f32[3,1,32,64]{3,2,1,0:T(8,128)S(1)}, u32[]{:S(2)}, u32[]{:S(2)}) collective-permute-start(f32[3,1,32,64]{3,2,1,0:T(8,128)S(1)} %pad_maximum_fusion.8), channel_id=1, source_target_pairs={{1,0},{2,1},{3,2},{4,3},{5,4},{6,5},{7,6},{9,8},{10,9},{11,10},{12... | collective-permute-start | bytes 73736 | tf_op jit(solution)/shard_map/ppermute | solution.py:19
  38.6 6.4 %collective-permute-start.6 = (f32[3,1,32,64]{3,2,1,0:T(8,128)S(1)}, f32[3,1,32,64]{3,2,1,0:T(8,128)S(1)}, u32[]{:S(2)}, u32[]{:S(2)}) collective-permute-start(f32[3,1,32,64]{3,2,1,0:T(8,128)S(1)} %pad_maximum_fusion.8), channel_id=1, source_target_pairs={{0,1},{1,2},{2,3},{3,4},{4,5},{5,6},{6,7},{8,9},{9,10},{10,11},{11... | collective-permute-start | bytes 73736 | tf_op jit(solution)/shard_map/ppermute | solution.py:17
  206.9 5.8 %collective-permute-start.9 = (f32[1,1,32,64]{3,2,1,0:T(8,128)S(1)}, f32[1,1,32,64]{3,2,1,0:T(8,128)S(1)}, u32[]{:S(2)}, u32[]{:S(2)}) collective-permute-start(f32[1,1,32,64]{3,2,1,0:T(8,128)S(1)} %bitcast.113), channel_id=1, source_target_pairs={{8,0},{16,8},{24,16},{32,24},{40,32},{48,40},{56,48},{64,56},{72,6... | collective-permute-start | bytes 24584 | tf_op jit(solution)/shard_map/ppermute | solution.py:19
  210.8 7.8 %collective-permute-start.8 = (f32[1,1,32,64]{3,2,1,0:T(8,128)S(1)}, f32[1,1,32,64]{3,2,1,0:T(8,128)S(1)}, u32[]{:S(2)}, u32[]{:S(2)}) collective-permute-start(f32[1,1,32,64]{3,2,1,0:T(8,128)S(1)} %bitcast.114), channel_id=1, source_target_pairs={{0,8},{8,16},{16,24},{24,32},{32,40},{40,48},{48,56},{56,64},{64,7... | collective-permute-start | bytes 24584 | tf_op jit(solution)/shard_map/ppermute | solution.py:17
  218.6 5.9 %collective-permute-start.11 = (f32[3,1,32,64]{3,2,1,0:T(8,128)S(1)}, f32[3,1,32,64]{3,2,1,0:T(8,128)S(1)}, u32[]{:S(2)}, u32[]{:S(2)}) collective-permute-start(f32[3,1,32,64]{3,2,1,0:T(8,128)S(1)} %pad_maximum_fusion.9), channel_id=1, source_target_pairs={{1,0},{2,1},{3,2},{4,3},{5,4},{6,5},{7,6},{9,8},{10,9},{11,10},{12... | collective-permute-start | bytes 73736 | tf_op jit(solution)/shard_map/ppermute | solution.py:19
  226.0 5.3 collective-permute-start.13
  227.9 7.8 %collective-permute-start.12 = (f32[1,1,32,64]{3,2,1,0:T(8,128)S(1)}, f32[1,1,32,64]{3,2,1,0:T(8,128)S(1)}, u32[]{:S(2)}, u32[]{:S(2)}) collective-permute-start(f32[1,1,32,64]{3,2,1,0:T(8,128)S(1)} %convolution_bitcast_fusion.1), channel_id=1, source_target_pairs={{0,8},{8,16},{16,24},{24,32},{32,40},{40,48},{48,56},{56,64},{64,7... | collective-permute-start | bytes 24584 | tf_op jit(solution)/shard_map/ppermute | solution.py:17
  235.7 7.5 %collective-permute-start.15 = (f32[3,1,32,64]{3,2,1,0:T(8,128)S(1)}, f32[3,1,32,64]{3,2,1,0:T(8,128)S(1)}, u32[]{:S(2)}, u32[]{:S(2)}) collective-permute-start(f32[3,1,32,64]{3,2,1,0:T(8,128)S(1)} %pad_maximum_fusion.10), channel_id=1, source_target_pairs={{1,0},{2,1},{3,2},{4,3},{5,4},{6,5},{7,6},{9,8},{10,9},{11,10},{12... | collective-permute-start | bytes 73736 | tf_op jit(solution)/shard_map/ppermute | solution.py:19
  238.9 5.2 collective-permute-start.14
  402.4 6.2 %collective-permute-start.17 = (f32[1,1,32,64]{3,2,1,0:T(8,128)S(1)}, f32[1,1,32,64]{3,2,1,0:T(8,128)S(1)}, u32[]{:S(2)}, u32[]{:S(2)}) collective-permute-start(f32[1,1,32,64]{3,2,1,0:T(8,128)S(1)} %bitcast.109), channel_id=1, source_target_pairs={{8,0},{16,8},{24,16},{32,24},{40,32},{48,40},{56,48},{64,56},{72,6... | collective-permute-start | bytes 24584 | tf_op jit(solution)/shard_map/ppermute | solution.py:19
  406.6 7.8 %collective-permute-start.16 = (f32[1,1,32,64]{3,2,1,0:T(8,128)S(1)}, f32[1,1,32,64]{3,2,1,0:T(8,128)S(1)}, u32[]{:S(2)}, u32[]{:S(2)}) collective-permute-start(f32[1,1,32,64]{3,2,1,0:T(8,128)S(1)} %bitcast.110), channel_id=1, source_target_pairs={{0,8},{8,16},{16,24},{24,32},{32,40},{40,48},{48,56},{56,64},{64,7... | collective-permute-start | bytes 24584 | tf_op jit(solution)/shard_map/ppermute | solution.py:17
  414.5 5.9 %collective-permute-start.19 = (f32[3,1,32,64]{3,2,1,0:T(8,128)S(1)}, f32[3,1,32,64]{3,2,1,0:T(8,128)S(1)}, u32[]{:S(2)}, u32[]{:S(2)}) collective-permute-start(f32[3,1,32,64]{3,2,1,0:T(8,128)S(1)} %pad_maximum_fusion.11), channel_id=1, source_target_pairs={{1,0},{2,1},{3,2},{4,3},{5,4},{6,5},{7,6},{9,8},{10,9},{11,10},{12... | collective-permute-start | bytes 73736 | tf_op jit(solution)/shard_map/ppermute | solution.py:19
  421.8 5.3 collective-permute-start.21
  423.7 7.8 %collective-permute-start.20 = (f32[1,1,32,64]{3,2,1,0:T(8,128)S(1)}, f32[1,1,32,64]{3,2,1,0:T(8,128)S(1)}, u32[]{:S(2)}, u32[]{:S(2)}) collective-permute-start(f32[1,1,32,64]{3,2,1,0:T(8,128)S(1)} %convolution_bitcast_fusion), channel_id=1, source_target_pairs={{0,8},{8,16},{16,24},{24,32},{32,40},{40,48},{48,56},{56,64},{64,7... | collective-permute-start | bytes 24584 | tf_op jit(solution)/shard_map/ppermute | solution.py:17
  431.6 7.3 %collective-permute-start.23 = (f32[3,1,32,64]{3,2,1,0:T(8,128)S(1)}, f32[3,1,32,64]{3,2,1,0:T(8,128)S(1)}, u32[]{:S(2)}, u32[]{:S(2)}) collective-permute-start(f32[3,1,32,64]{3,2,1,0:T(8,128)S(1)} %pad_maximum_fusion.12), channel_id=1, source_target_pairs={{1,0},{2,1},{3,2},{4,3},{5,4},{6,5},{7,6},{9,8},{10,9},{11,10},{12... | collective-permute-start | bytes 73736 | tf_op jit(solution)/shard_map/ppermute | solution.py:19
  434.8 5.2 collective-permute-start.22
  523.5 5.6 %collective-permute-start.25 = (f32[1,1,32,64]{3,2,1,0:T(8,128)S(1)}, f32[1,1,32,64]{3,2,1,0:T(8,128)S(1)}, u32[]{:S(2)}, u32[]{:S(2)}) collective-permute-start(f32[1,1,32,64]{3,2,1,0:T(8,128)S(1)} %bitcast.105), channel_id=1, source_target_pairs={{8,0},{16,8},{24,16},{32,24},{40,32},{48,40},{56,48},{64,56},{72,6... | collective-permute-start | bytes 24584 | tf_op jit(solution)/shard_map/ppermute | solution.py:19
  527.2 7.8 %collective-permute-start.24 = (f32[1,1,32,64]{3,2,1,0:T(8,128)S(1)}, f32[1,1,32,64]{3,2,1,0:T(8,128)S(1)}, u32[]{:S(2)}, u32[]{:S(2)}) collective-permute-start(f32[1,1,32,64]{3,2,1,0:T(8,128)S(1)} %bitcast.106), channel_id=1, source_target_pairs={{0,8},{8,16},{16,24},{24,32},{32,40},{40,48},{48,56},{56,64},{64,7... | collective-permute-start | bytes 24584 | tf_op jit(solution)/shard_map/ppermute | solution.py:17
  535.0 7.7 %collective-permute-start.27 = (f32[3,1,32,64]{3,2,1,0:T(8,128)S(1)}, f32[3,1,32,64]{3,2,1,0:T(8,128)S(1)}, u32[]{:S(2)}, u32[]{:S(2)}) collective-permute-start(f32[3,1,32,64]{3,2,1,0:T(8,128)S(1)} %pad_maximum_fusion.13), channel_id=1, source_target_pairs={{1,0},{2,1},{3,2},{4,3},{5,4},{6,5},{7,6},{9,8},{10,9},{11,10},{12... | collective-permute-start | bytes 73736 | tf_op jit(solution)/shard_map/ppermute | solution.py:19
  (12 other events, 443.5 us)
where the time goes:
time: 563 us; the launch traced here: 561 us
  blocking collectives  381 us (68%)
  starting transfers between devices  87.6 us (16%)
  waiting for transfers between devices  43.8 us (8%)
  matrix products  32 us (6%)
  between operations  7.94 us (1%)
    psum x3, blocking collectives, squares(): return lax.psum(jnp.sum(values * values), ('gx', 'gy'))  221 us
    psum x2, blocking collectives, per_device(): alpha = norm_now / lax.psum(jnp.sum(direction * image), ('gx', 'gy'))  146 us
    ppermute x14, starting transfers between devices, with_halo(): lax.ppermute(head, axis, [((i + 1) % count, i) for i in range(ends)])  45.9 us
    ppermute x14, waiting for transfers between devices, with_halo(): lax.ppermute(tail, axis, [(i, (i + 1) % count) for i in range(ends)])  43.8 us
    ppermute x14, starting transfers between devices, with_halo(): lax.ppermute(tail, axis, [(i, (i + 1) % count) for i in range(ends)])  41.7 us
    dot_general x4, matrix products, coefficient(): jnp.einsum('bfv,bv->bf', features, field, precision=lax.Precision.HIGHEST)  22 us
    all_gather x1, blocking collectives, per_device(): slab_rows = lax.all_gather(surface, 'gy', axis=0, tiled=True)  13.1 us
  transfers between devices with their start and end apart: 28, of which 14 were waited for; matrix products, arithmetic and copies ran while one was open for 0% of the time, Pallas kernels for 0%

commit v1 on v0

--- a/solution.py
+++ b/solution.py
@@ -1,9 +1,18 @@
+import functools
 import jax
 import jax.numpy as jnp
 from jax import lax
 from jax.sharding import PartitionSpec as P
 
 ITERS = 3
+
+
+def lane_detail(u_in, a_name):
+    t1 = jnp.concatenate([u_in] * lax.psum(1, a_name), axis=0)
+    return lax.all_to_all(t1, a_name, 0, 0, tiled=True)
+
+
+put_copies = functools.partial(lane_detail, a_name="gy")
 
 
 def with_halo(cells, sides, width):
@@ -78,7 +87,7 @@
         direction = residual + norm_next / norm_now * direction
         norm_now = norm_next
     surface = first_sum(coefficient(features, solution_field))
-    slab_rows = lax.all_gather(surface, "gy", axis=0, tiled=True)
+    slab_rows = put_copies(surface)
     local_ids = vertex_bricks - row_index * across * nrows
     picked = jnp.take(slab_rows, local_ids, axis=0)
     vertex_values = jnp.sum(vertex_features * picked.T, axis=0)

time: 563 us -> 562 us (level)
  blocking collectives: 381 us -> 368 us
    all_gather x1 -> x0, blocking collectives: 13.1 us -> none  [per_device(): slab_rows = lax.all_gather(surface, 'gy', axis=0, tiled=True)]
  transfers between devices with their start and end apart: 28 -> 29, of which waited for: 14 -> 15; matrix products, arithmetic and copies ran while one was open for 0% -> 0% of each run, Pallas kernels for 0% -> 0%
where the time goes in v1:
time: 562 us; the launch traced here: 559 us
  blocking collectives  368 us (65%)
  starting transfers between devices  92.1 us (16%)
  waiting for transfers between devices  48.7 us (9%)
  matrix products  32 us (6%)
  between operations  8 us (1%)
  other arithmetic  6.12 us (1%)
    psum x3, blocking collectives, squares(): return lax.psum(jnp.sum(values * values), ('gx', 'gy'))  221 us
    psum x2, blocking collectives, per_device(): alpha = norm_now / lax.psum(jnp.sum(direction * image), ('gx', 'gy'))  146 us
    ppermute x14, starting transfers between devices, with_halo(): lax.ppermute(head, axis, [((i + 1) % count, i) for i in range(ends)])  45.9 us
    ppermute x14, waiting for transfers between devices, with_halo(): lax.ppermute(tail, axis, [(i, (i + 1) % count) for i in range(ends)])  44 us
    ppermute x14, starting transfers between devices, with_halo(): lax.ppermute(tail, axis, [(i, (i + 1) % count) for i in range(ends)])  41.7 us
    dot_general x4, matrix products, coefficient(): jnp.einsum('bfv,bv->bf', features, field, precision=lax.Precision.HIGHEST)  22 us
  transfers between devices with their start and end apart: 29, of which 15 were waited for; matrix products, arithmetic and copies ran while one was open for 0% of the time, Pallas kernels for 0%

profile of v1, /device:TPU:129, one launch (start us, length us, event | category | flops | bytes accessed | tf_op | source)
XLA Modules:
  0.0 559.1 jit_solution(10469760436399397898)
XLA Ops:
  0.7 5.8 %fusion.8 = f32[32,1,64]{2,1,0:T(1,128)S(1)} fusion(f32[32,64,512]{2,1,0:T(8,128)} %param.8, f32[32,512,1]{1,0,2:T(8,128)} %bitcast.95), kind=kOutput, calls=%fused_computation.25 | convolution fusion | flops 12582912 | bytes 4268032 | tf_op jit(solution)/shard_map/bfv,bv->bf/dot_general | solution.py:36
  12.7 5.6 collective-permute-done
  18.2 4.0 collective-permute-start.3
  32.1 4.4 collective-permute-done.4
  38.6 5.2 collective-permute-start.6
  45.2 4.3 fusion.25
  50.2 74.5 %all-reduce = (f32[]{:T(128)}, f32[]{:T(128)}) all-reduce(f32[]{:T(128)} %get-tuple-element.4, f32[]{:T(128)} %get-tuple-element.3), channel_id=1, replica_groups=mesh['gx'=32,'gy'=8] {'gx','gy'}, use_global_device_ids=true, to_apply=%region_1.2 | all-reduce | flops 2 | bytes 16 | tf_op jit(solution)/shard_map/psum | solution.py:40
  126.7 73.5 %psum.44 = f32[]{:T(128)} all-reduce(f32[]{:T(128)} %get-tuple-element.9), channel_id=1, replica_groups=mesh['gx'=32,'gy'=8] {'gx','gy'}, use_global_device_ids=true, to_apply=%region_6.7 | all-reduce | flops 1 | bytes 8 | tf_op jit(solution)/shard_map/psum | solution.py:40
  201.5 5.4 fusion.6
  212.7 5.9 %collective-permute-done.8 = f32[1,1,32,64]{3,2,1,0:T(8,128)S(1)} collective-permute-done((f32[1,1,32,64]{3,2,1,0:T(8,128)S(1)}, f32[1,1,32,64]{3,2,1,0:T(8,128)S(1)}, u32[]{:S(2)}, u32[]{:S(2)}) %collective-permute-start.8) | collective-permute-done | bytes 8224 | tf_op jit(solution)/shard_map/ppermute | solution.py:26
  231.3 4.4 collective-permute-done.12
  238.9 4.3 collective-permute-start.14
  247.1 73.2 %psum.45 = f32[]{:T(128)} all-reduce(f32[]{:T(128)} %multiply_reduce_fusion.2), channel_id=1, replica_groups=mesh['gx'=32,'gy'=8] {'gx','gy'}, use_global_device_ids=true, to_apply=%region_8.9 | all-reduce | flops 1 | bytes 8 | tf_op jit(solution)/shard_map/psum | solution.py:83
  322.3 73.3 %psum.46 = f32[]{:T(128)} all-reduce(f32[]{:T(128)} %get-tuple-element.7), channel_id=1, replica_groups=mesh['gx'=32,'gy'=8] {'gx','gy'}, use_global_device_ids=true, to_apply=%region_10.11 | all-reduce | flops 1 | bytes 8 | tf_op jit(solution)/shard_map/psum | solution.py:40
  397.0 5.4 fusion.4
  402.4 4.2 collective-permute-start.17
  408.6 5.9 %collective-permute-done.16 = f32[1,1,32,64]{3,2,1,0:T(8,128)S(1)} collective-permute-done((f32[1,1,32,64]{3,2,1,0:T(8,128)S(1)}, f32[1,1,32,64]{3,2,1,0:T(8,128)S(1)}, u32[]{:S(2)}, u32[]{:S(2)}) %collective-permute-start.16) | collective-permute-done | bytes 8224 | tf_op jit(solution)/shard_map/ppermute | solution.py:26
  427.1 4.4 collective-permute-done.20
  434.8 4.1 collective-permute-start.22
  443.0 73.2 %psum.47 = f32[]{:T(128)} all-reduce(f32[]{:T(128)} %multiply_reduce_fusion), channel_id=1, replica_groups=mesh['gx'=32,'gy'=8] {'gx','gy'}, use_global_device_ids=true, to_apply=%region_12.13 | all-reduce | flops 1 | bytes 8 | tf_op jit(solution)/shard_map/psum | solution.py:83
  518.2 5.3 fusion.2
  529.1 5.9 %collective-permute-done.24 = f32[1,1,32,64]{3,2,1,0:T(8,128)S(1)} collective-permute-done((f32[1,1,32,64]{3,2,1,0:T(8,128)S(1)}, f32[1,1,32,64]{3,2,1,0:T(8,128)S(1)}, u32[]{:S(2)}, u32[]{:S(2)}) %collective-permute-start.24) | collective-permute-done | bytes 8224 | tf_op jit(solution)/shard_map/ppermute | solution.py:26
  544.7 4.4 all-to-all-start
  549.3 4.6 all-to-all-done
  (112 shorter events, 89.9 us)
Async XLA Ops:
  6.5 6.2 %collective-permute-start.1 = (f32[1,1,32,64]{3,2,1,0:T(8,128)S(1)}, f32[1,1,32,64]{3,2,1,0:T(8,128)S(1)}, u32[]{:S(2)}, u32[]{:S(2)}) collective-permute-start(f32[1,1,32,64]{3,2,1,0:T(8,128)S(1)} %bitcast.105), channel_id=1, source_target_pairs={{8,0},{16,8},{24,16},{32,24},{40,32},{48,40},{56,48},{64,56},{72,6... | collective-permute-start | bytes 24584 | tf_op jit(solution)/shard_map/ppermute | solution.py:28
  10.4 7.8 %collective-permute-start = (f32[1,1,32,64]{3,2,1,0:T(8,128)S(1)}, f32[1,1,32,64]{3,2,1,0:T(8,128)S(1)}, u32[]{:S(2)}, u32[]{:S(2)}) collective-permute-start(f32[1,1,32,64]{3,2,1,0:T(8,128)S(1)} %bitcast.106), channel_id=1, source_target_pairs={{0,8},{8,16},{16,24},{24,32},{32,40},{40,48},{48,56},{56,64},{64,7... | collective-permute-start | bytes 24584 | tf_op jit(solution)/shard_map/ppermute | solution.py:26
  18.2 7.4 %collective-permute-start.3 = (f32[3,1,32,64]{3,2,1,0:T(8,128)S(1)}, f32[3,1,32,64]{3,2,1,0:T(8,128)S(1)}, u32[]{:S(2)}, u32[]{:S(2)}) collective-permute-start(f32[3,1,32,64]{3,2,1,0:T(8,128)S(1)} %pad_maximum_fusion.7), channel_id=1, source_target_pairs={{1,0},{2,1},{3,2},{4,3},{5,4},{6,5},{7,6},{9,8},{10,9},{11,10},{12... | collective-permute-start | bytes 73736 | tf_op jit(solution)/shard_map/ppermute | solution.py:28
  26.8 5.3 collective-permute-start.5
  28.7 7.8 %collective-permute-start.4 = (f32[1,1,32,64]{3,2,1,0:T(8,128)S(1)}, f32[1,1,32,64]{3,2,1,0:T(8,128)S(1)}, u32[]{:S(2)}, u32[]{:S(2)}) collective-permute-start(f32[1,1,32,64]{3,2,1,0:T(8,128)S(1)} %convolution_bitcast_fusion.2), channel_id=1, source_target_pairs={{0,8},{8,16},{16,24},{24,32},{32,40},{40,48},{48,56},{56,64},{64,7... | collective-permute-start | bytes 24584 | tf_op jit(solution)/shard_map/ppermute | solution.py:26
  36.5 7.3 %collective-permute-start.7 = (f32[3,1,32,64]{3,2,1,0:T(8,128)S(1)}, f32[3,1,32,64]{3,2,1,0:T(8,128)S(1)}, u32[]{:S(2)}, u32[]{:S(2)}) collective-permute-start(f32[3,1,32,64]{3,2,1,0:T(8,128)S(1)} %pad_maximum_fusion.8), channel_id=1, source_target_pairs={{1,0},{2,1},{3,2},{4,3},{5,4},{6,5},{7,6},{9,8},{10,9},{11,10},{12... | collective-permute-start | bytes 73736 | tf_op jit(solution)/shard_map/ppermute | solution.py:28
  38.6 6.4 %collective-permute-start.6 = (f32[3,1,32,64]{3,2,1,0:T(8,128)S(1)}, f32[3,1,32,64]{3,2,1,0:T(8,128)S(1)}, u32[]{:S(2)}, u32[]{:S(2)}) collective-permute-start(f32[3,1,32,64]{3,2,1,0:T(8,128)S(1)} %pad_maximum_fusion.8), channel_id=1, source_target_pairs={{0,1},{1,2},{2,3},{3,4},{4,5},{5,6},{6,7},{8,9},{9,10},{10,11},{11... | collective-permute-start | bytes 73736 | tf_op jit(solution)/shard_map/ppermute | solution.py:26
  206.9 5.8 %collective-permute-start.9 = (f32[1,1,32,64]{3,2,1,0:T(8,128)S(1)}, f32[1,1,32,64]{3,2,1,0:T(8,128)S(1)}, u32[]{:S(2)}, u32[]{:S(2)}) collective-permute-start(f32[1,1,32,64]{3,2,1,0:T(8,128)S(1)} %bitcast.117), channel_id=1, source_target_pairs={{8,0},{16,8},{24,16},{32,24},{40,32},{48,40},{56,48},{64,56},{72,6... | collective-permute-start | bytes 24584 | tf_op jit(solution)/shard_map/ppermute | solution.py:28
  210.8 7.8 %collective-permute-start.8 = (f32[1,1,32,64]{3,2,1,0:T(8,128)S(1)}, f32[1,1,32,64]{3,2,1,0:T(8,128)S(1)}, u32[]{:S(2)}, u32[]{:S(2)}) collective-permute-start(f32[1,1,32,64]{3,2,1,0:T(8,128)S(1)} %bitcast.118), channel_id=1, source_target_pairs={{0,8},{8,16},{16,24},{24,32},{32,40},{40,48},{48,56},{56,64},{64,7... | collective-permute-start | bytes 24584 | tf_op jit(solution)/shard_map/ppermute | solution.py:26
  218.6 5.9 %collective-permute-start.11 = (f32[3,1,32,64]{3,2,1,0:T(8,128)S(1)}, f32[3,1,32,64]{3,2,1,0:T(8,128)S(1)}, u32[]{:S(2)}, u32[]{:S(2)}) collective-permute-start(f32[3,1,32,64]{3,2,1,0:T(8,128)S(1)} %pad_maximum_fusion.9), channel_id=1, source_target_pairs={{1,0},{2,1},{3,2},{4,3},{5,4},{6,5},{7,6},{9,8},{10,9},{11,10},{12... | collective-permute-start | bytes 73736 | tf_op jit(solution)/shard_map/ppermute | solution.py:28
  226.0 5.3 collective-permute-start.13
  227.9 7.8 %collective-permute-start.12 = (f32[1,1,32,64]{3,2,1,0:T(8,128)S(1)}, f32[1,1,32,64]{3,2,1,0:T(8,128)S(1)}, u32[]{:S(2)}, u32[]{:S(2)}) collective-permute-start(f32[1,1,32,64]{3,2,1,0:T(8,128)S(1)} %convolution_bitcast_fusion.1), channel_id=1, source_target_pairs={{0,8},{8,16},{16,24},{24,32},{32,40},{40,48},{48,56},{56,64},{64,7... | collective-permute-start | bytes 24584 | tf_op jit(solution)/shard_map/ppermute | solution.py:26
  235.7 7.5 %collective-permute-start.15 = (f32[3,1,32,64]{3,2,1,0:T(8,128)S(1)}, f32[3,1,32,64]{3,2,1,0:T(8,128)S(1)}, u32[]{:S(2)}, u32[]{:S(2)}) collective-permute-start(f32[3,1,32,64]{3,2,1,0:T(8,128)S(1)} %pad_maximum_fusion.10), channel_id=1, source_target_pairs={{1,0},{2,1},{3,2},{4,3},{5,4},{6,5},{7,6},{9,8},{10,9},{11,10},{12... | collective-permute-start | bytes 73736 | tf_op jit(solution)/shard_map/ppermute | solution.py:28
  238.9 5.2 collective-permute-start.14
  402.4 6.2 %collective-permute-start.17 = (f32[1,1,32,64]{3,2,1,0:T(8,128)S(1)}, f32[1,1,32,64]{3,2,1,0:T(8,128)S(1)}, u32[]{:S(2)}, u32[]{:S(2)}) collective-permute-start(f32[1,1,32,64]{3,2,1,0:T(8,128)S(1)} %bitcast.113), channel_id=1, source_target_pairs={{8,0},{16,8},{24,16},{32,24},{40,32},{48,40},{56,48},{64,56},{72,6... | collective-permute-start | bytes 24584 | tf_op jit(solution)/shard_map/ppermute | solution.py:28
  406.6 7.8 %collective-permute-start.16 = (f32[1,1,32,64]{3,2,1,0:T(8,128)S(1)}, f32[1,1,32,64]{3,2,1,0:T(8,128)S(1)}, u32[]{:S(2)}, u32[]{:S(2)}) collective-permute-start(f32[1,1,32,64]{3,2,1,0:T(8,128)S(1)} %bitcast.114), channel_id=1, source_target_pairs={{0,8},{8,16},{16,24},{24,32},{32,40},{40,48},{48,56},{56,64},{64,7... | collective-permute-start | bytes 24584 | tf_op jit(solution)/shard_map/ppermute | solution.py:26
  414.4 5.9 %collective-permute-start.19 = (f32[3,1,32,64]{3,2,1,0:T(8,128)S(1)}, f32[3,1,32,64]{3,2,1,0:T(8,128)S(1)}, u32[]{:S(2)}, u32[]{:S(2)}) collective-permute-start(f32[3,1,32,64]{3,2,1,0:T(8,128)S(1)} %pad_maximum_fusion.11), channel_id=1, source_target_pairs={{1,0},{2,1},{3,2},{4,3},{5,4},{6,5},{7,6},{9,8},{10,9},{11,10},{12... | collective-permute-start | bytes 73736 | tf_op jit(solution)/shard_map/ppermute | solution.py:28
  421.8 5.3 collective-permute-start.21
  423.7 7.8 %collective-permute-start.20 = (f32[1,1,32,64]{3,2,1,0:T(8,128)S(1)}, f32[1,1,32,64]{3,2,1,0:T(8,128)S(1)}, u32[]{:S(2)}, u32[]{:S(2)}) collective-permute-start(f32[1,1,32,64]{3,2,1,0:T(8,128)S(1)} %convolution_bitcast_fusion), channel_id=1, source_target_pairs={{0,8},{8,16},{16,24},{24,32},{32,40},{40,48},{48,56},{56,64},{64,7... | collective-permute-start | bytes 24584 | tf_op jit(solution)/shard_map/ppermute | solution.py:26
  431.5 7.3 %collective-permute-start.23 = (f32[3,1,32,64]{3,2,1,0:T(8,128)S(1)}, f32[3,1,32,64]{3,2,1,0:T(8,128)S(1)}, u32[]{:S(2)}, u32[]{:S(2)}) collective-permute-start(f32[3,1,32,64]{3,2,1,0:T(8,128)S(1)} %pad_maximum_fusion.12), channel_id=1, source_target_pairs={{1,0},{2,1},{3,2},{4,3},{5,4},{6,5},{7,6},{9,8},{10,9},{11,10},{12... | collective-permute-start | bytes 73736 | tf_op jit(solution)/shard_map/ppermute | solution.py:28
  523.5 5.6 %collective-permute-start.25 = (f32[1,1,32,64]{3,2,1,0:T(8,128)S(1)}, f32[1,1,32,64]{3,2,1,0:T(8,128)S(1)}, u32[]{:S(2)}, u32[]{:S(2)}) collective-permute-start(f32[1,1,32,64]{3,2,1,0:T(8,128)S(1)} %bitcast.109), channel_id=1, source_target_pairs={{8,0},{16,8},{24,16},{32,24},{40,32},{48,40},{56,48},{64,56},{72,6... | collective-permute-start | bytes 24584 | tf_op jit(solution)/shard_map/ppermute | solution.py:28
  527.2 7.8 %collective-permute-start.24 = (f32[1,1,32,64]{3,2,1,0:T(8,128)S(1)}, f32[1,1,32,64]{3,2,1,0:T(8,128)S(1)}, u32[]{:S(2)}, u32[]{:S(2)}) collective-permute-start(f32[1,1,32,64]{3,2,1,0:T(8,128)S(1)} %bitcast.110), channel_id=1, source_target_pairs={{0,8},{8,16},{16,24},{24,32},{32,40},{40,48},{48,56},{56,64},{64,7... | collective-permute-start | bytes 24584 | tf_op jit(solution)/shard_map/ppermute | solution.py:26
  535.0 7.5 %collective-permute-start.27 = (f32[3,1,32,64]{3,2,1,0:T(8,128)S(1)}, f32[3,1,32,64]{3,2,1,0:T(8,128)S(1)}, u32[]{:S(2)}, u32[]{:S(2)}) collective-permute-start(f32[3,1,32,64]{3,2,1,0:T(8,128)S(1)} %pad_maximum_fusion.13), channel_id=1, source_target_pairs={{1,0},{2,1},{3,2},{4,3},{5,4},{6,5},{7,6},{9,8},{10,9},{11,10},{12... | collective-permute-start | bytes 73736 | tf_op jit(solution)/shard_map/ppermute | solution.py:28
  544.7 9.3 %all-to-all-start = ((f32[8,1,2048]{2,1,0:T(1,128)}), f32[8,1,2048]{2,1,0:T(1,128)S(1)}, u32[]{:S(2)}, u32[]{:S(2)}) async-start(f32[8,1,2048]{2,1,0:T(1,128)} %reshape.94), calls=%async_computation | async-start | bytes 131072 | tf_op jit(solution)/shard_map/all_to_all | solution.py:12
  (13 other events, 467.1 us)
